TPU v7x, 256 devices: a whole 4x4x8 slice. The times are simulated.
256 devices in a mesh: ia: 4 (over x), ja: 8 (over z_hi, y), ka: 8 (over z_lo, core).
Axes of the slice: x: 4, y: 4, z: 8 (z_hi: 2, z_lo: 4; z = z_hi * 4 + z_lo), core: 2. Of those that a mesh axis runs over, the one named last changes fastest.
Arguments:
- tensor: bfloat16 [1024, 1024, 1024], P('ia', 'ja', 'ka'), may hold values from -6 to 6
- factor_b: bfloat16 [1024, 256], P('ja', 'ka'), may hold values from -16 to 16
- factor_c: bfloat16 [1024, 256], P('ka', 'ja'), may hold values from -16 to 16
Outputs:
- factor_a: float32 [1024, 256], P(('ia', 'ja', 'ka'))
All inputs are finite; a program needn't handle non-finite values.
Results may differ from a plain program's by a relative error of at most 0.0003.
Values may be sent and summed in bfloat16 or wider, within the bound.
A program may use at most 64 MiB of HBM per device.

v0:
```python
import math

import jax
import jax.numpy as jnp
from jax import lax
from jax.sharding import Mesh
from jax.sharding import PartitionSpec as P

KA = ("ka_0", "ka_1")
JA = ("ja_0", "ja_1")
JA_KA = ("ja_0", "ja_1", "ka_0", "ka_1")
IA_JA_KA = ("ia", "ja_0", "ja_1", "ka_0", "ka_1")


ridge_weight = 0.1


def laid_out(pieces, dim):
    pieces = jnp.moveaxis(pieces, 0, dim)
    dims = pieces.shape
    return pieces.reshape(*dims[:dim], dims[dim] * dims[dim + 1], *dims[dim + 2 :])


def sent_to_all(x, axis):
    copies = jnp.broadcast_to(x, (lax.axis_size(axis), *x.shape))
    return lax.all_to_all(copies, axis, split_axis=0, concat_axis=0, tiled=True)


def collect(x, axis, dim):
    return laid_out(sent_to_all(x, axis), dim)


def rows_for(lines, length):
    spare = -len(lines) % length
    return jnp.pad(lines, [(0, spare)] + [(0, 0)] * (lines.ndim - 1))


def gathered_by_axis(x, axes, dim):
    far, near = axes
    first = sent_to_all(x, far)
    pieces = jnp.swapaxes(sent_to_all(first, near), 0, 1)
    return laid_out(pieces.reshape(-1, *x.shape), dim)


def cut_along(x, dim, length):
    dims = x.shape
    pieces = x.reshape(*dims[:dim], length, dims[dim] // length, *dims[dim + 1 :])
    return jnp.moveaxis(pieces, dim, 0)


def sum_at_owner(x, axis, dim):
    pieces = cut_along(x, dim, lax.axis_size(axis))
    arrived = lax.all_to_all(pieces, axis, split_axis=0, concat_axis=0, tiled=True)
    return arrived.sum(axis=0)


def sum_in_two_steps(x, axes, dim):
    far, near = axes
    own = sum_at_owner(cut_along(x, dim, lax.axis_size(far)), near, dim + 1)
    return jnp.sum(lax.all_to_all(own, far, 0, 0, tiled=True), axis=0)


def nested_sum(x, axes):
    padded = rows_for(x, lax.axis_size(axes[0]) * lax.axis_size(axes[1]))
    whole = gathered_by_axis(sum_in_two_steps(padded, axes, 0), axes, 0)
    return lax.slice_in_dim(whole, 0, len(x)).reshape(x.shape)


def together(arrays, axis):
    flat, at, done = (jnp.concatenate([a.reshape(-1) for a in arrays]), 0, [])
    so_far = nested_sum(flat, axis)
    for a in arrays:
        done.append(so_far[at : at + a.size].reshape(a.shape))
        at += a.size
    return tuple(done)


def contract(block, b_wide, c_wide):
    rows, width_j, width_k = block.shape
    inner = jnp.dot(
        block.reshape(rows * width_j, width_k), c_wide, preferred_element_type=jnp.float32
    )
    inner = inner.reshape(rows, width_j, -1)
    return jnp.sum(inner * b_wide.astype(jnp.float32)[None], axis=1)


def partial_rows(tensor, b_wide, c_wide, row_count):
    step_rows = math.gcd(row_count, 16)
    pieces = tensor.reshape(row_count // step_rows, step_rows, tensor.shape[1], tensor.shape[2])
    result = lax.map(lambda piece: contract(piece, b_wide, c_wide), pieces)
    return result.reshape(row_count, b_wide.shape[1])


def body(tensor, factor_b, factor_c):
    b_wide = collect(factor_b, KA, 1)
    c_wide = collect(factor_c, JA, 1)
    rank = b_wide.shape[1]
    rows_b = b_wide.shape[0] // lax.axis_size(KA)
    rows_c = c_wide.shape[0] // lax.axis_size(JA)
    piece_b = lax.dynamic_slice_in_dim(b_wide, lax.axis_index(KA) * rows_b, rows_b, 0)
    piece_c = lax.dynamic_slice_in_dim(c_wide, lax.axis_index(JA) * rows_c, rows_c, 0)
    gram_b, gram_c = together(
        (
            jnp.dot(piece_b.T, piece_b, preferred_element_type=jnp.float32),
            jnp.dot(piece_c.T, piece_c, preferred_element_type=jnp.float32),
        ),
        (("ja_0", "ja_1", "ka_0"), "ka_1"),
    )
    normal_matrix = gram_b * gram_c + ridge_weight * jnp.eye(rank, dtype=jnp.float32)
    block_rows = tensor.shape[0]
    owned = block_rows // (lax.axis_size(JA) * lax.axis_size(KA))
    mine = sum_in_two_steps(
        partial_rows(tensor, b_wide, c_wide, owned * lax.axis_size(JA_KA)),
        (("ja_0", "ja_1", "ka_0"), "ka_1"),
        0,
    )
    lower = jnp.linalg.cholesky(normal_matrix)
    solved = jax.scipy.linalg.cho_solve((lower, True), mine.T)
    return solved.T


def solution(mesh):
    torus = Mesh(
        mesh.devices.reshape(mesh.shape["ia"], 2, 4, 4, 2), ("ia", "ja_0", "ja_1", "ka_0", "ka_1")
    )
    return jax.shard_map(
        body,
        mesh=torus,
        in_specs=(P("ia", JA, KA), P(JA, KA), P(KA, JA)),
        out_specs=P(IA_JA_KA, None),
        check_vma=False,
    )
```

profile of v0, /device:TPU:1, one launch (start us, length us, event | category | flops | bytes accessed | tf_op | source)
XLA Modules:
  0.0 185.6 jit_solution(17702929862796534568)
XLA Ops:
  0.0 1.3 broadcast_in_dim.22
  1.3 7.4 %all-to-all-start = ((bf16[8,128,32]{1,2,0:T(8,128)(2,1)}), bf16[8,128,32]{1,2,0:T(8,128)(2,1)S(1)}, u32[]{:S(2)}, u32[]{:S(2)}) async-start(bf16[8,128,32]{1,2,0:T(8,128)(2,1)} %broadcast_in_dim.22), calls=%async_computation | async-start | bytes 131072 | tf_op jit(solution)/shard_map/all_to_all | solution.py:26
  8.7 5.1 %all-to-all-done = bf16[8,128,32]{1,2,0:T(8,128)(2,1)S(1)} async-done(((bf16[8,128,32]{1,2,0:T(8,128)(2,1)}), bf16[8,128,32]{1,2,0:T(8,128)(2,1)S(1)}, u32[]{:S(2)}, u32[]{:S(2)}) %all-to-all-start) | async-done | bytes 65568 | tf_op jit(solution)/shard_map/all_to_all | solution.py:26
  13.8 1.3 broadcast_in_dim.23
  15.1 8.2 %all-to-all-start.1 = ((bf16[8,128,32]{1,2,0:T(8,128)(2,1)}), bf16[8,128,32]{1,2,0:T(8,128)(2,1)S(1)}, u32[]{:S(2)}, u32[]{:S(2)}) async-start(bf16[8,128,32]{1,2,0:T(8,128)(2,1)} %broadcast_in_dim.23), calls=%async_computation.1 | async-start | bytes 131072 | tf_op jit(solution)/shard_map/all_to_all | solution.py:26
  23.4 0.3 fusion.10
  23.7 0.2 concatenate.14
  23.9 0.2 copy.54
  24.0 8.5 %all-to-all-done.1 = bf16[8,128,32]{1,2,0:T(8,128)(2,1)S(1)} async-done(((bf16[8,128,32]{1,2,0:T(8,128)(2,1)}), bf16[8,128,32]{1,2,0:T(8,128)(2,1)S(1)}, u32[]{:S(2)}, u32[]{:S(2)}) %all-to-all-start.1) | async-done | bytes 65568 | tf_op jit(solution)/shard_map/all_to_all | solution.py:26
  32.6 0.3 fusion.8
  32.9 0.2 concatenate.15
  33.0 0.2 copy.55
  33.2 6.0 %all_to_all.48 = f32[2,32,2048]{2,1,0:T(8,128)S(1)} all-to-all(f32[2,32,2048]{2,1,0:T(8,128)S(1)} %maximum_bitcast_fusion), channel_id=1, replica_groups=mesh['ia'=4,'ja_0'=2,'ja_1'=4,'ka_0'=4,'ka_1'=2] {'ka_1'}, dimensions={0} | all-to-all | bytes 1048576 | tf_op jit(solution)/shard_map/all_to_all | solution.py:53
  39.3 0.9 all_to_all.33
  40.2 24.5 %while.11 = (s32[]{:T(128)}, f32[16,16,256]{2,1,0:T(8,128)S(1)}, bf16[16,16,128,128]{3,2,1,0:T(8,128)(2,1)}, bf16[128,256]{1,0:T(8,128)(2,1)S(1)}, bf16[128,256]{1,0:T(8,128)(2,1)S(1)}, /*index=5*/s32[]{:T(128)}) while((s32[]{:T(128)}, f32[16,16,256]{2,1,0:T(8,128)S(1)}, bf16[16,16,128,128]{3,2,1,0:T(8,128)(2,1)}, ...), condition=%wide.region_8.9_spmd, body=%wide.region_6.8_spmd.sunk | while | flops 135294976 | bytes 967241 | solution.py:90
  40.2 1.5 multiply_reduce_fusion.2
  41.7 1.5 multiply_reduce_fusion.2
  43.2 1.5 multiply_reduce_fusion.2
  44.8 1.5 multiply_reduce_fusion.2
  46.3 1.5 multiply_reduce_fusion.2
  47.8 1.5 multiply_reduce_fusion.2
  49.4 1.5 multiply_reduce_fusion.2
  50.9 1.5 multiply_reduce_fusion.2
  52.4 1.5 multiply_reduce_fusion.2
  54.0 1.5 multiply_reduce_fusion.2
  55.5 1.5 multiply_reduce_fusion.2
  57.0 1.5 multiply_reduce_fusion.2
  58.6 1.5 multiply_reduce_fusion.2
  60.1 1.5 multiply_reduce_fusion.2
  61.6 1.5 multiply_reduce_fusion.2
  63.2 1.5 multiply_reduce_fusion.2
  64.8 3.8 %all_to_all.49 = f32[2,32,4,256]{3,2,1,0:T(4,128)S(1)} all-to-all(f32[2,32,4,256]{3,2,1,0:T(4,128)S(1)} %copy.65), channel_id=1, replica_groups=mesh['ia'=4,'ja_0'=2,'ja_1'=4,'ka_0'=4,'ka_1'=2] {'ka_1'}, dimensions={0} | all-to-all | bytes 524288 | tf_op jit(solution)/shard_map/all_to_all | solution.py:53
  68.6 3.9 %all-to-all-start.3 = ((f32[32,1,2048]{2,1,0:T(1,128)}), f32[32,1,2048]{2,1,0:T(1,128)S(1)}, u32[]{:S(2)}, u32[]{:S(2)}) async-start(f32[32,1,2048]{2,1,0:T(1,128)} %all_to_all.33), calls=%async_computation.3 | async-start | bytes 524288 | tf_op jit(solution)/shard_map/all_to_all | solution.py:60
  72.5 0.7 reduce_sum.47
  73.2 11.9 %all-to-all-done.3 = f32[32,1,2048]{2,1,0:T(1,128)S(1)} async-done(((f32[32,1,2048]{2,1,0:T(1,128)}), f32[32,1,2048]{2,1,0:T(1,128)S(1)}, u32[]{:S(2)}, u32[]{:S(2)}) %all-to-all-start.3) | async-done | bytes 262176 | tf_op jit(solution)/shard_map/all_to_all | solution.py:60
  85.1 3.8 %all-to-all-start.7 = ((f32[32,4,256]{2,1,0:T(4,128)}), f32[32,4,256]{2,1,0:T(4,128)S(1)}, u32[]{:S(2)}, u32[]{:S(2)}) async-start(f32[32,4,256]{2,1,0:T(4,128)} %reduce_sum.47), calls=%async_computation.7 | async-start | bytes 262144 | tf_op jit(solution)/shard_map/all_to_all | solution.py:60
  89.0 0.2 reduce_sum.46
  89.1 9.6 %all-to-all-done.7 = f32[32,4,256]{2,1,0:T(4,128)S(1)} async-done(((f32[32,4,256]{2,1,0:T(4,128)}), f32[32,4,256]{2,1,0:T(4,128)S(1)}, u32[]{:S(2)}, u32[]{:S(2)}) %all-to-all-start.7) | async-done | bytes 131104 | tf_op jit(solution)/shard_map/all_to_all | solution.py:60
  98.8 0.8 broadcast_in_dim.24
  99.6 3.9 %all-to-all-start.4 = ((f32[32,1,2048]{2,1,0:T(1,128)}), f32[32,1,2048]{2,1,0:T(1,128)S(1)}, u32[]{:S(2)}, u32[]{:S(2)}) async-start(f32[32,1,2048]{2,1,0:T(1,128)} %broadcast_in_dim.24), calls=%async_computation.4 | async-start | bytes 524288 | tf_op jit(solution)/shard_map/all_to_all | solution.py:26
  103.5 10.9 %all-to-all-done.4 = f32[32,1,2048]{2,1,0:T(1,128)S(1)} async-done(((f32[32,1,2048]{2,1,0:T(1,128)}), f32[32,1,2048]{2,1,0:T(1,128)S(1)}, u32[]{:S(2)}, u32[]{:S(2)}) %all-to-all-start.4) | async-done | bytes 262176 | tf_op jit(solution)/shard_map/all_to_all | solution.py:26
  114.6 7.9 %all_to_all.50 = f32[2,32,2048]{2,1,0:T(8,128)S(1)} all-to-all(f32[2,32,2048]{2,1,0:T(8,128)S(1)} %broadcast_in_dim.25), channel_id=1, replica_groups=mesh['ia'=4,'ja_0'=2,'ja_1'=4,'ka_0'=4,'ka_1'=2] {'ka_1'}, dimensions={0} | all-to-all | bytes 1048576 | tf_op jit(solution)/shard_map/all_to_all | solution.py:26
  122.6 0.2 copy.56
  122.8 0.2 mul.37
  123.0 0.1 copy.57
  123.4 11.7 %cholesky.49 = f32[128,128]{1,0:T(8,128)S(1)} custom-call(f32[128,128]{1,0:T(8,128)S(1)} %cholesky.115), custom_call_target="Cholesky" | custom-call | tf_op jit(solution)/shard_map/jit(cholesky)/cholesky | solution.py:117
  135.1 9.8 %custom-call.18 = f32[1,128,128]{1,2,0:T(8,128)S(1)} custom-call(f32[1,128,128]{2,1,0:T(8,128)S(1)} %get-tuple-element.111), custom_call_target="InvertDiagBlocksLowerTriangular" | custom-call | tf_op jit(solution)/shard_map/jit(cholesky)/cholesky | solution.py:117
  144.9 0.2 fusion.5
  145.1 0.3 convolution_subtract_fusion
  145.4 11.7 %cholesky.103 = f32[128,128]{1,0:T(8,128)S(1)} custom-call(f32[128,128]{1,0:T(8,128)S(1)} %convolution_subtract_fusion), custom_call_target="Cholesky" | custom-call | tf_op jit(solution)/shard_map/jit(cholesky)/cholesky | solution.py:117
  157.5 0.7 compare_reduce_fusion
  159.6 4.3 %while.12 = (s32[]{:T(128)}, f32[256,256]{0,1:T(8,128)S(1)}, s32[2,2]{1,0:T(2,128)S(1)}, f32[2,128,128]{2,1,0:T(8,128)S(1)}, s32[]{:T(128)}) while((s32[]{:T(128)}, f32[256,256]{0,1:T(8,128)S(1)}, s32[2,2]{1,0:T(2,128)S(1)}, f32[2,128,128]{2,1,0:T(8,128)S(1)}, s32[]{:T(128)}) %tuple.45), condition=%wide.while_cond, body=%wide.while_body.sunk | while | flops 2 | bytes 393321 | solution.py:118
  159.6 0.7 fusion.34
  160.3 1.3 dynamic-slice.7
  161.8 0.7 fusion.34
  162.4 1.3 dynamic-slice.7
  163.9 19.9 %custom-call.19 = f32[2,128,128]{1,2,0:T(8,128)S(1)} custom-call(f32[2,128,128]{2,1,0:T(8,128)S(1)} %get-tuple-element.40), custom_call_target="InvertDiagBlocksLowerTriangular" | custom-call | tf_op jit(solution)/shard_map/jit(_cho_solve)/triangular_solve | solution.py:118
  183.8 0.2 fusion.13
  183.9 0.2 convolution_subtract_fusion.2
  184.1 0.2 fusion.15
  184.3 0.2 fusion.14
  184.5 0.2 convolution_subtract_fusion.1
  184.7 0.2 fusion.12
  184.9 0.6 maximum_bitcast_fusion.1
  (65 shorter events, 1.8 us)
Async XLA Ops:
  1.3 12.4 %all-to-all-start = ((bf16[8,128,32]{1,2,0:T(8,128)(2,1)}), bf16[8,128,32]{1,2,0:T(8,128)(2,1)S(1)}, u32[]{:S(2)}, u32[]{:S(2)}) async-start(bf16[8,128,32]{1,2,0:T(8,128)(2,1)} %broadcast_in_dim.22), calls=%async_computation | async-start | bytes 131072 | tf_op jit(solution)/shard_map/all_to_all | solution.py:26
  15.1 17.4 %all-to-all-start.1 = ((bf16[8,128,32]{1,2,0:T(8,128)(2,1)}), bf16[8,128,32]{1,2,0:T(8,128)(2,1)S(1)}, u32[]{:S(2)}, u32[]{:S(2)}) async-start(bf16[8,128,32]{1,2,0:T(8,128)(2,1)} %broadcast_in_dim.23), calls=%async_computation.1 | async-start | bytes 131072 | tf_op jit(solution)/shard_map/all_to_all | solution.py:26
  68.6 16.5 %all-to-all-start.3 = ((f32[32,1,2048]{2,1,0:T(1,128)}), f32[32,1,2048]{2,1,0:T(1,128)S(1)}, u32[]{:S(2)}, u32[]{:S(2)}) async-start(f32[32,1,2048]{2,1,0:T(1,128)} %all_to_all.33), calls=%async_computation.3 | async-start | bytes 524288 | tf_op jit(solution)/shard_map/all_to_all | solution.py:60
  85.1 13.6 %all-to-all-start.7 = ((f32[32,4,256]{2,1,0:T(4,128)}), f32[32,4,256]{2,1,0:T(4,128)S(1)}, u32[]{:S(2)}, u32[]{:S(2)}) async-start(f32[32,4,256]{2,1,0:T(4,128)} %reduce_sum.47), calls=%async_computation.7 | async-start | bytes 262144 | tf_op jit(solution)/shard_map/all_to_all | solution.py:60
  99.6 14.9 %all-to-all-start.4 = ((f32[32,1,2048]{2,1,0:T(1,128)}), f32[32,1,2048]{2,1,0:T(1,128)S(1)}, u32[]{:S(2)}, u32[]{:S(2)}) async-start(f32[32,1,2048]{2,1,0:T(1,128)} %broadcast_in_dim.24), calls=%async_computation.4 | async-start | bytes 524288 | tf_op jit(solution)/shard_map/all_to_all | solution.py:26
where the time goes:
time: 187 us; the launch traced here: 186 us
  other arithmetic  55.9 us (30%)
  waiting for transfers between devices  46 us (25%)
  starting transfers between devices  27.2 us (15%)
  matrix products  25.7 us (14%)
  blocking collectives  17.7 us (9%)
  local copies, waits for them, and re-layouts  10.8 us (6%)
    another operation x6, other arithmetic, body(): lower = jnp.linalg.cholesky(normal_matrix)  34 us
    all_to_all x3, waiting for transfers between devices, sent_to_all(): return lax.all_to_all(copies, axis, split_axis=0, concat_axis=0, tiled=True)  24.4 us
    dot_general x16, matrix products, contract(): jnp.dot(block.reshape(rows * width_j, width_k), c_wide, preferred_element...  23.6 us
    all_to_all x2, waiting for transfers between devices, sum_in_two_steps(): return jnp.sum(lax.all_to_all(own, far, 0, 0, tiled=True), axis=0)  21.5 us
    another operation x3, other arithmetic, body(): solved = jax.scipy.linalg.cho_solve((lower, True), mine.T)  19.9 us
    all_to_all x3, starting transfers between devices, sent_to_all(): return lax.all_to_all(copies, axis, split_axis=0, concat_axis=0, tiled=True)  19.5 us
    all_to_all x2, blocking collectives, sum_at_owner(): lax.all_to_all(pieces, axis, split_axis=0, concat_axis=0, tiled=True)  9.82 us
    all_to_all x1, blocking collectives, sent_to_all(): return lax.all_to_all(copies, axis, split_axis=0, concat_axis=0, tiled=True)  7.92 us
  transfers between devices with their start and end apart: 5, of which 5 were waited for; matrix products, arithmetic and copies ran while one was open for 1% of the time, Pallas kernels for 0%

commit v1 on v0

v1 whole, which is shorter than its diff:
```python
import jax
import jax.numpy as jnp
from jax import lax
from jax.experimental import pallas as pl
from jax.experimental.pallas import tpu as pltpu
from jax.sharding import PartitionSpec as P

MESH = pl.DeviceIdType.MESH
RIDGE = 0.1
GROUP = 8
PLANE = GROUP * GROUP
RANK = 256
LANES = 128
SUB = 8
BLOCK = 16
ROWS = 256
DEPTH = 128
STEP = 8
CHUNKS = 8


def split3(x):
    a = x.astype(jnp.bfloat16)
    rest = x - a.astype(jnp.float32)
    b = rest.astype(jnp.bfloat16)
    c = (rest - b.astype(jnp.float32)).astype(jnp.bfloat16)
    return a, b, c


def eliminate(a_ref, cols_ref, w_ref, lhs_ref, rhs_ref):
    lane8 = lax.broadcasted_iota(jnp.int32, (SUB, LANES), 1)
    lane_n = lax.broadcasted_iota(jnp.int32, (RANK, LANES), 1)

    def step(t, carry):
        half = t // SUB
        off = lax.rem(t, SUB) * BLOCK
        rows = pl.ds(pl.multiple_of(t * BLOCK, BLOCK), BLOCK)
        d = a_ref[half, rows, :]
        d = pltpu.roll(d, lax.rem(LANES - off, LANES), 1)
        for j in range(BLOCK):
            cols_ref[j] = jnp.broadcast_to(d[:, j : j + 1], (BLOCK, LANES))
        s, low, inv, y = {}, {}, [], []
        for j in range(BLOCK):
            for i in range(j, BLOCK):
                s[i, j] = cols_ref[j, pl.ds(i, SUB, stride=0), :]
        for i in range(BLOCK):
            eye = jnp.where(lane8 == off + i, -1.0, 0.0)
            row = []
            for h in range(2):
                inside = (lane8 >= off) & (lane8 < off + BLOCK) & (half == h)
                row.append(jnp.where(inside, eye, a_ref[h, pl.ds(t * BLOCK + i, SUB, stride=0), :]))
            y.append(row)
        for k in range(BLOCK):
            inv.append(pltpu.reciprocal(s[k, k]))
            for j in range(k + 1, BLOCK):
                low[j, k] = s[j, k] * inv[k]
            for j in range(k + 1, BLOCK):
                for i in range(j, BLOCK):
                    s[i, j] = s[i, j] - low[i, k] * s[j, k]
                for h in range(2):
                    y[j][h] = y[j][h] - low[j, k] * y[k][h]
        for k in range(BLOCK):
            for h in range(2):
                y[k][h] = y[k][h] * inv[k]
        for k in range(BLOCK - 1, -1, -1):
            for h in range(2):
                w_ref[h, k : k + 1, :] = y[k][h][0:1]
            for j in range(k):
                for h in range(2):
                    y[j][h] = y[j][h] - low[k, j] * y[k][h]
        for h in range(2):
            lanes = pl.ds(h * LANES, LANES)
            r1, r2, r3 = split3(a_ref[h, rows, :])
            lhs_ref[:, lanes] = jnp.concatenate([r1, r1, r2, r2, r1, r3], axis=0)
            w1, w2, w3 = split3(w_ref[h])
            rhs_ref[:, lanes] = jnp.concatenate([w1, w2, w1, w2, w3, w1], axis=0)
        change = lax.dot_general(
            lhs_ref[...], rhs_ref[...], (((0,), (0,)), ((), ())), preferred_element_type=jnp.float32
        )
        for h in range(2):
            inside = (lane_n >= off) & (lane_n < off + BLOCK) & (half == h)
            a_ref[h] = jnp.where(inside, 0.0, a_ref[h]) - change[:, h * LANES : (h + 1) * LANES]
        for h in range(2):
            a_ref[h, rows, :] = w_ref[h]
        return carry

    lax.fori_loop(0, RANK // BLOCK, step, 0)


def kernel(
    t_hbm, fb_ref, fc_ref, out_ref,
    t_buf, b_buf, c_buf, b_wide, c_wide, gb, gc, gb_in, gc_in, a_ref, m_out, m_in,
    cols_ref, w_ref, lhs_ref, rhs_ref,
    t_sem, b_send, b_recv, c_send, c_recv, gb_send, gb_recv, gc_send, gc_recv,
    a_send, a_recv, m_send, m_recv,
):
    ja = lax.axis_index("ja")
    ka = lax.axis_index("ka")
    me = ja * GROUP + ka

    def load(n):
        span = pl.ds(n * (ROWS // CHUNKS), ROWS // CHUNKS)
        return pltpu.make_async_copy(t_hbm.at[span], t_buf.at[span], t_sem.at[n])

    for n in range(CHUNKS):
        load(n).start()

    barrier = pltpu.get_barrier_semaphore()

    def greet(d, carry):
        q = lax.rem(me + d, PLANE)
        pl.semaphore_signal(
            barrier, inc=1, device_id={"ja": q // GROUP, "ka": lax.rem(q, GROUP)}, device_id_type=MESH
        )
        return carry

    lax.fori_loop(1, PLANE, greet, 0)
    b_buf[ka] = fb_ref[...].astype(jnp.float32).T.astype(jnp.bfloat16)
    c_buf[ja] = fc_ref[...].astype(jnp.float32).T.astype(jnp.bfloat16)
    pl.semaphore_wait(barrier, PLANE - 1)

    def remote(src, dst, send, recv, device):
        return pltpu.make_async_remote_copy(
            src_ref=src, dst_ref=dst, send_sem=send, recv_sem=recv, device_id=device, device_id_type=MESH
        )

    def b_copy(d):
        return remote(b_buf.at[ka], b_buf.at[ka], b_send.at[d], b_recv.at[d], {"ka": lax.rem(ka + d, GROUP)})

    def c_copy(d):
        return remote(c_buf.at[ja], c_buf.at[ja], c_send.at[d], c_recv.at[d], {"ja": lax.rem(ja + d, GROUP)})

    def b_landed(d):
        slot = lax.rem(ka + GROUP - d, GROUP)
        return remote(b_buf.at[slot], b_buf.at[slot], b_send.at[d], b_recv.at[d], {"ka": slot})

    def c_landed(d):
        slot = lax.rem(ja + GROUP - d, GROUP)
        return remote(c_buf.at[slot], c_buf.at[slot], c_send.at[d], c_recv.at[d], {"ja": slot})

    for d in range(1, GROUP):
        c_copy(d).start()
        b_copy(d).start()

    for d in range(1, GROUP):
        b_landed(d).wait_recv()
    bt = b_buf[...].reshape(RANK, DEPTH)
    nt = (((1,), (1,)), ((), ()))
    gram = lax.dot_general(bt, bt, nt, preferred_element_type=jnp.float32)
    for h in range(2):
        gb[pl.ds(h * 32, 32)] = gram[:, h * LANES : (h + 1) * LANES].reshape(32, SUB, LANES)

    def gb_copy(d):
        q = lax.rem(ja + d, GROUP)
        return remote(gb.at[q * GROUP + ka], gb_in.at[ja], gb_send.at[d], gb_recv.at[d], {"ja": q})

    def gb_landed(d):
        q = lax.rem(ja + GROUP - d, GROUP)
        return remote(gb.at[q * GROUP + ka], gb_in.at[q], gb_send.at[d], gb_recv.at[d], {"ja": q})

    for d in range(1, GROUP):
        gb_copy(d).start()
    gb_in[ja] = gb[ja * GROUP + ka]

    for d in range(1, GROUP):
        c_landed(d).wait_recv()
    ct = c_buf[...].reshape(RANK, DEPTH)
    gram = lax.dot_general(ct, ct, nt, preferred_element_type=jnp.float32)
    for h in range(2):
        gc[pl.ds(h * 32, 32)] = gram[:, h * LANES : (h + 1) * LANES].reshape(32, SUB, LANES)

    def gc_copy(d):
        q = lax.rem(ka + d, GROUP)
        return remote(gc.at[ja * GROUP + q], gc_in.at[ka], gc_send.at[d], gc_recv.at[d], {"ka": q})

    def gc_landed(d):
        q = lax.rem(ka + GROUP - d, GROUP)
        return remote(gc.at[ja * GROUP + q], gc_in.at[q], gc_send.at[d], gc_recv.at[d], {"ka": q})

    for d in range(1, GROUP):
        gc_copy(d).start()
    gc_in[ka] = gc[ja * GROUP + ka]

    b_wide[...] = bt.astype(jnp.float32).T
    c_wide[...] = ct.astype(jnp.float32).T.astype(jnp.bfloat16)

    def contract(n, carry):
        x = t_buf[pl.ds(n * STEP, STEP)].reshape(STEP * DEPTH, DEPTH)
        inner = jnp.dot(x, c_wide[...], preferred_element_type=jnp.float32)
        total = jnp.sum(inner.reshape(STEP, DEPTH, RANK) * b_wide[...][None], axis=1)
        left, right = total[:, :LANES], total[:, LANES:]
        m_out[2 * n] = jnp.concatenate([left[:4], right[:4]], axis=0)
        m_out[2 * n + 1] = jnp.concatenate([left[4:], right[4:]], axis=0)
        return carry

    steps = ROWS // STEP
    per_chunk = steps // CHUNKS
    for n in range(CHUNKS // 2):
        load(n).wait()
        lax.fori_loop(n * per_chunk, (n + 1) * per_chunk, contract, 0)

    for d in range(1, GROUP):
        gb_landed(d).wait_recv()
        gc_landed(d).wait_recv()
    sum_b = jnp.sum(gb_in[...], axis=0)
    sum_c = jnp.sum(gc_in[...], axis=0)
    my_half = me // 32
    my_row = lax.rem(me, 32) * SUB
    row = lax.broadcasted_iota(jnp.int32, (SUB, LANES), 0) + my_row
    col = lax.broadcasted_iota(jnp.int32, (SUB, LANES), 1) + my_half * LANES
    mine = pl.ds(pl.multiple_of(my_row, SUB), SUB)
    a_ref[my_half, mine, :] = sum_b * sum_c + jnp.where(row == col, RIDGE, 0.0)

    def place(q):
        return {"ja": q // GROUP, "ka": lax.rem(q, GROUP)}

    def tile(q):
        return a_ref.at[q // 32, pl.ds(pl.multiple_of(lax.rem(q, 32) * SUB, SUB), SUB), :]

    def a_copy(d):
        return remote(tile(me), tile(me), a_send.at[d], a_recv.at[d], place(lax.rem(me + d, PLANE)))

    def a_landed(d):
        q = lax.rem(me + PLANE - d, PLANE)
        return remote(tile(q), tile(q), a_send.at[d], a_recv.at[d], place(q))

    def m_copy(d):
        q = lax.rem(me + d, PLANE)
        return remote(m_out.at[q], m_in.at[me], m_send.at[d], m_recv.at[d], place(q))

    def m_landed(d):
        q = lax.rem(me + PLANE - d, PLANE)
        return remote(m_out.at[q], m_in.at[q], m_send.at[d], m_recv.at[d], place(q))

    def each(action):
        def body(d, carry):
            action(d)
            return carry

        lax.fori_loop(1, PLANE, body, 0)

    each(lambda d: a_copy(d).start())
    for n in range(CHUNKS // 2, CHUNKS):
        load(n).wait()
        lax.fori_loop(n * per_chunk, (n + 1) * per_chunk, contract, 0)
    each(lambda d: a_landed(d).wait_recv())
    each(lambda d: m_copy(d).start())
    each(lambda d: a_copy(d).wait_send())
    m_in[me] = m_out[me]

    eliminate(a_ref, cols_ref, w_ref, lhs_ref, rhs_ref)

    each(lambda d: m_landed(d).wait_recv())
    total = jnp.sum(m_in[...], axis=0)
    left, right = total[:4], total[4:]
    for h in range(2):
        part = jnp.dot(left, a_ref[h, pl.ds(0, LANES), :], precision=lax.Precision.HIGHEST,
                       preferred_element_type=jnp.float32)
        part += jnp.dot(right, a_ref[h, pl.ds(LANES, LANES), :], precision=lax.Precision.HIGHEST,
                        preferred_element_type=jnp.float32)
        out_ref[:, h * LANES : (h + 1) * LANES] = -part

    for d in range(1, GROUP):
        b_copy(d).wait_send()
        c_copy(d).wait_send()
        gb_copy(d).wait_send()
        gc_copy(d).wait_send()
    each(lambda d: m_copy(d).wait_send())


def body(tensor, factor_b, factor_c):
    f32, bf16 = jnp.float32, jnp.bfloat16
    vmem, dma = pltpu.VMEM, pltpu.SemaphoreType.DMA
    return pl.pallas_call(
        kernel,
        out_shape=jax.ShapeDtypeStruct((4, RANK), f32),
        in_specs=[
            pl.BlockSpec(memory_space=pl.ANY),
            pl.BlockSpec(memory_space=pltpu.VMEM),
            pl.BlockSpec(memory_space=pltpu.VMEM),
        ],
        out_specs=pl.BlockSpec(memory_space=pltpu.VMEM),
        scratch_shapes=[
            vmem((ROWS, DEPTH, DEPTH), bf16),
            vmem((GROUP, RANK // GROUP, DEPTH), bf16),
            vmem((GROUP, RANK // GROUP, DEPTH), bf16),
            vmem((DEPTH, RANK), f32),
            vmem((DEPTH, RANK), bf16),
            vmem((PLANE, SUB, LANES), f32),
            vmem((PLANE, SUB, LANES), f32),
            vmem((GROUP, SUB, LANES), f32),
            vmem((GROUP, SUB, LANES), f32),
            vmem((2, RANK, LANES), f32),
            vmem((PLANE, SUB, LANES), f32),
            vmem((PLANE, SUB, LANES), f32),
            vmem((BLOCK, BLOCK, LANES), f32),
            vmem((2, BLOCK, LANES), f32),
            vmem((6 * BLOCK, RANK), bf16),
            vmem((6 * BLOCK, RANK), bf16),
            dma((CHUNKS,)),
            *[dma((GROUP,)) for _ in range(8)],
            *[dma((PLANE,)) for _ in range(4)],
        ],
        compiler_params=pltpu.CompilerParams(collective_id=0, has_side_effects=True),
        name="factor_update",
    )(tensor, factor_b, factor_c)


def solution(mesh):
    return jax.shard_map(
        body,
        mesh=mesh,
        in_specs=(P("ia", "ja", "ka"), P("ja", "ka"), P("ka", "ja")),
        out_specs=P(("ia", "ja", "ka"), None),
        check_vma=False,
    )
```

time: 187 us -> 54.8 us (0.29)
  other arithmetic: 55.9 us -> 0 us
  Pallas kernels: 0 us -> 50.4 us
  waiting for transfers between devices: 46 us -> 0 us
  starting transfers between devices: 27.2 us -> 0 us
  matrix products: 25.7 us -> 0 us
  blocking collectives: 17.7 us -> 0 us
  local copies, waits for them, and re-layouts: 10.8 us -> 4.07 us
    another operation x9 -> x0, other arithmetic: 54 us -> none  [the longest x6 34 us: body(): lower = jnp.linalg.cholesky(normal_matrix)]
    pallas_call x0 -> x1, Pallas kernels: none -> 50.4 us  [body(): pl.pallas_call(kernel, out_shape=jax.ShapeDtypeStruct((4, RANK), f32), in...]
    all_to_all x5 -> x0, waiting for transfers between devices: 46 us -> none  [the longest x3 24.4 us: sent_to_all(): return lax.all_to_all(copies, axis, split_axis=0, concat_axis=0, tiled=True)]
    all_to_all x5 -> x0, starting transfers between devices: 27.2 us -> none  [the longest x3 19.5 us: sent_to_all(): return lax.all_to_all(copies, axis, split_axis=0, concat_axis=0, tiled=True)]
    dot_general x18 -> x0, matrix products: 24.1 us -> none  [the longest x16 23.6 us: contract(): jnp.dot(block.reshape(rows * width_j, width_k), c_wide, preferred_element...]
    all_to_all x3 -> x0, blocking collectives: 17.7 us -> none  [the longest x2 9.82 us: sum_at_owner(): lax.all_to_all(pieces, axis, split_axis=0, concat_axis=0, tiled=True)]
    another operation x19 -> x0, local copies, waits for them, and re-layouts: 4.69 us -> none
    unnamed x1 -> x3, local copies, waits for them, and re-layouts: 0.08 us -> 4.07 us
  transfers between devices with their start and end apart: 5 -> 0, of which waited for: 5 -> 0; matrix products, arithmetic and copies ran while one was open for 1% -> 0% of each run, Pallas kernels for 0% -> 0%
where the time goes in v1:
time: 54.8 us; the launch traced here: 54.5 us
  Pallas kernels  50.4 us (92%)
  local copies, waits for them, and re-layouts  4.07 us (7%)
    pallas_call x1, Pallas kernels, body(): pl.pallas_call(kernel, out_shape=jax.ShapeDtypeStruct((4, RANK), f32), in...  50.4 us
    unnamed x3, local copies, waits for them, and re-layouts  4.07 us

profile of v1, /device:TPU:1, one launch (start us, length us, event | category | flops | bytes accessed | tf_op | source)
XLA Modules:
  0.0 54.5 jit_solution(7188574736599955325)
XLA Ops:
  0.0 1.4 %copy.4.fb_ref = bf16[128,32]{1,0:T(8,128)(2,1)} copy(bf16[128,32]{0,1:T(8,128)(2,1)} %param.4) | data formatting | bytes 16384 | tf_op args[1]
  1.4 1.4 %copy.5.fc_ref = bf16[128,32]{1,0:T(8,128)(2,1)} copy(bf16[128,32]{0,1:T(8,128)(2,1)} %param.5) | data formatting | bytes 16384 | tf_op args[2]
  2.8 50.4 %factor_update.1 = f32[4,256]{1,0:T(4,128)} custom-call(bf16[256,128,128]{2,1,0:T(8,128)(2,1)} %t_hbm.1, bf16[128,32]{1,0:T(8,128)(2,1)} %copy.4.fb_ref, bf16[128,32]{1,0:T(8,128)(2,1)} %copy.5.fc_ref), custom_call_target="tpu_custom_call" | custom-call | tf_op jit(solution)/shard_map/factor_update/pallas_call | solution.py:274
  53.2 1.3 %copy.7 = f32[4,256]{1,0:T(4,128)} copy(f32[4,256]{1,0:T(4,128)} %factor_update.1) | data formatting | bytes 8192

commit v2 on v1

--- a/solution.py
+++ b/solution.py
@@ -27,7 +27,7 @@
     return a, b, c
 
 
-def eliminate(a_ref, cols_ref, w_ref, lhs_ref, rhs_ref):
+def eliminate(first, last, a_ref, cols_ref, w_ref, lhs_ref, rhs_ref):
     lane8 = lax.broadcasted_iota(jnp.int32, (SUB, LANES), 1)
     lane_n = lax.broadcasted_iota(jnp.int32, (RANK, LANES), 1)
 
@@ -84,40 +84,55 @@
             a_ref[h, rows, :] = w_ref[h]
         return carry
 
-    lax.fori_loop(0, RANK // BLOCK, step, 0)
+    lax.fori_loop(first, last, step, 0)
 
 
 def kernel(
-    t_hbm, fb_ref, fc_ref, out_ref,
-    t_buf, b_buf, c_buf, b_wide, c_wide, gb, gc, gb_in, gc_in, a_ref, m_out, m_in,
+    t_hbm, fb_hbm, fc_hbm, out_ref,
+    t_buf, b_buf, c_buf, b_wide, c_wide, gb, gc, gb_in, gc_in, a_ref, m_out, my_in, mz_out, mz_in,
     cols_ref, w_ref, lhs_ref, rhs_ref,
-    t_sem, b_send, b_recv, c_send, c_recv, gb_send, gb_recv, gc_send, gc_recv,
-    a_send, a_recv, m_send, m_recv,
+    f_sem, t_sem, b_send, b_recv, c_send, c_recv, gb_send, gb_recv, gc_send, gc_recv,
+    az_send, az_recv, ay_send, ay_recv, my_send, my_recv, mz_send, mz_recv,
 ):
     ja = lax.axis_index("ja")
     ka = lax.axis_index("ka")
-    me = ja * GROUP + ka
+    y, core, z = lax.rem(ja, 4), lax.rem(ka, 2), (ja // 4) * 4 + ka // 2
+    column = y * 2 + core
+
+    def along_z(p):
+        return {"ja": (p // 4) * 4 + y, "ka": lax.rem(p, 4) * 2 + core}
+
+    def along_y(p):
+        return {"ja": (ja // 4) * 4 + p // 2, "ka": (ka // 2) * 2 + lax.rem(p, 2)}
+
+    def tile_of(j, k):
+        return (lax.rem(j, 4) * 2 + lax.rem(k, 2)) * GROUP + (j // 4) * 4 + k // 2
+
+    me = tile_of(ja, ka)
 
     def load(n):
         span = pl.ds(n * (ROWS // CHUNKS), ROWS // CHUNKS)
         return pltpu.make_async_copy(t_hbm.at[span], t_buf.at[span], t_sem.at[n])
 
+    load_b = pltpu.make_async_copy(fb_hbm, b_buf.at[ka], f_sem.at[0])
+    load_c = pltpu.make_async_copy(fc_hbm, c_buf.at[ja], f_sem.at[1])
+    load_b.start()
+    load_c.start()
     for n in range(CHUNKS):
         load(n).start()
 
     barrier = pltpu.get_barrier_semaphore()
 
-    def greet(d, carry):
-        q = lax.rem(me + d, PLANE)
-        pl.semaphore_signal(
-            barrier, inc=1, device_id={"ja": q // GROUP, "ka": lax.rem(q, GROUP)}, device_id_type=MESH
-        )
-        return carry
-
-    lax.fori_loop(1, PLANE, greet, 0)
-    b_buf[ka] = fb_ref[...].astype(jnp.float32).T.astype(jnp.bfloat16)
-    c_buf[ja] = fc_ref[...].astype(jnp.float32).T.astype(jnp.bfloat16)
-    pl.semaphore_wait(barrier, PLANE - 1)
+    partners = [{"ja": lax.rem(ja + d, GROUP)} for d in range(1, GROUP)]
+    partners += [{"ka": lax.rem(ka + d, GROUP)} for d in range(1, GROUP)]
+    partners += [{"ja": lax.rem(ja + 4, GROUP), "ka": lax.rem(ka + 2 * d, GROUP)} for d in range(1, 4)]
+    other = ka + 1 - 2 * core
+    partners += [{"ja": (ja // 4) * 4 + lax.rem(y + d, 4), "ka": other} for d in range(1, 4)]
+    for partner in partners:
+        pl.semaphore_signal(barrier, inc=1, device_id=partner, device_id_type=MESH)
+    load_b.wait()
+    load_c.wait()
+    pl.semaphore_wait(barrier, len(partners))
 
     def remote(src, dst, send, recv, device):
         return pltpu.make_async_remote_copy(
@@ -152,15 +167,15 @@
 
     def gb_copy(d):
         q = lax.rem(ja + d, GROUP)
-        return remote(gb.at[q * GROUP + ka], gb_in.at[ja], gb_send.at[d], gb_recv.at[d], {"ja": q})
+        return remote(gb.at[tile_of(q, ka)], gb_in.at[ja], gb_send.at[d], gb_recv.at[d], {"ja": q})
 
     def gb_landed(d):
         q = lax.rem(ja + GROUP - d, GROUP)
-        return remote(gb.at[q * GROUP + ka], gb_in.at[q], gb_send.at[d], gb_recv.at[d], {"ja": q})
+        return remote(gb.at[tile_of(q, ka)], gb_in.at[q], gb_send.at[d], gb_recv.at[d], {"ja": q})
 
     for d in range(1, GROUP):
         gb_copy(d).start()
-    gb_in[ja] = gb[ja * GROUP + ka]
+    gb_in[ja] = gb[me]
 
     for d in range(1, GROUP):
         c_landed(d).wait_recv()
@@ -171,15 +186,15 @@
 
     def gc_copy(d):
         q = lax.rem(ka + d, GROUP)
-        return remote(gc.at[ja * GROUP + q], gc_in.at[ka], gc_send.at[d], gc_recv.at[d], {"ka": q})
+        return remote(gc.at[tile_of(ja, q)], gc_in.at[ka], gc_send.at[d], gc_recv.at[d], {"ka": q})
 
     def gc_landed(d):
         q = lax.rem(ka + GROUP - d, GROUP)
-        return remote(gc.at[ja * GROUP + q], gc_in.at[q], gc_send.at[d], gc_recv.at[d], {"ka": q})
+        return remote(gc.at[tile_of(ja, q)], gc_in.at[q], gc_send.at[d], gc_recv.at[d], {"ka": q})
 
     for d in range(1, GROUP):
         gc_copy(d).start()
-    gc_in[ka] = gc[ja * GROUP + ka]
+    gc_in[ka] = gc[me]
 
     b_wide[...] = bt.astype(jnp.float32).T
     c_wide[...] = ct.astype(jnp.float32).T.astype(jnp.bfloat16)
@@ -189,8 +204,9 @@
         inner = jnp.dot(x, c_wide[...], preferred_element_type=jnp.float32)
         total = jnp.sum(inner.reshape(STEP, DEPTH, RANK) * b_wide[...][None], axis=1)
         left, right = total[:, :LANES], total[:, LANES:]
-        m_out[2 * n] = jnp.concatenate([left[:4], right[:4]], axis=0)
-        m_out[2 * n + 1] = jnp.concatenate([left[4:], right[4:]], axis=0)
+        j, k = n // 4, lax.rem(n, 4) * 2
+        m_out[tile_of(j, k)] = jnp.concatenate([left[:4], right[:4]], axis=0)
+        m_out[tile_of(j, k + 1)] = jnp.concatenate([left[4:], right[4:]], axis=0)
         return carry
 
     steps = ROWS // STEP
@@ -211,47 +227,78 @@
     mine = pl.ds(pl.multiple_of(my_row, SUB), SUB)
     a_ref[my_half, mine, :] = sum_b * sum_c + jnp.where(row == col, RIDGE, 0.0)
 
-    def place(q):
-        return {"ja": q // GROUP, "ka": lax.rem(q, GROUP)}
-
-    def tile(q):
-        return a_ref.at[q // 32, pl.ds(pl.multiple_of(lax.rem(q, 32) * SUB, SUB), SUB), :]
-
-    def a_copy(d):
-        return remote(tile(me), tile(me), a_send.at[d], a_recv.at[d], place(lax.rem(me + d, PLANE)))
-
-    def a_landed(d):
-        q = lax.rem(me + PLANE - d, PLANE)
-        return remote(tile(q), tile(q), a_send.at[d], a_recv.at[d], place(q))
-
-    def m_copy(d):
-        q = lax.rem(me + d, PLANE)
-        return remote(m_out.at[q], m_in.at[me], m_send.at[d], m_recv.at[d], place(q))
-
-    def m_landed(d):
-        q = lax.rem(me + PLANE - d, PLANE)
-        return remote(m_out.at[q], m_in.at[q], m_send.at[d], m_recv.at[d], place(q))
-
-    def each(action):
-        def body(d, carry):
-            action(d)
-            return carry
-
-        lax.fori_loop(1, PLANE, body, 0)
-
-    each(lambda d: a_copy(d).start())
+    def part(ref, p):
+        return ref.at[p // 4, pl.ds(pl.multiple_of(lax.rem(p, 4) * 64, 64), 64), :]
+
+    def az_tile(p):
+        start = lax.rem(column, 4) * 64 + p * SUB
+        return a_ref.at[column // 4, pl.ds(pl.multiple_of(start, SUB), SUB), :]
+
+    def az_copy(d):
+        return remote(az_tile(z), az_tile(z), az_send.at[d], az_recv.at[d], along_z(lax.rem(z + d, GROUP)))
+
+    def az_landed(d):
+        p = lax.rem(z + GROUP - d, GROUP)
+        return remote(az_tile(p), az_tile(p), az_send.at[d], az_recv.at[d], along_z(p))
+
+    def ay_copy(d):
+        return remote(
+            part(a_ref, column), part(a_ref, column), ay_send.at[d], ay_recv.at[d], along_y(lax.rem(column + d, GROUP))
+        )
+
+    def ay_landed(d):
+        p = lax.rem(column + GROUP - d, GROUP)
+        return remote(part(a_ref, p), part(a_ref, p), ay_send.at[d], ay_recv.at[d], along_y(p))
+
+    def my_copy(d):
+        p = lax.rem(column + d, GROUP)
+        return remote(
+            m_out.at[pl.ds(p * GROUP, GROUP)], my_in.at[column], my_send.at[d], my_recv.at[d], along_y(p)
+        )
+
+    def my_landed(d):
+        p = lax.rem(column + GROUP - d, GROUP)
+        return remote(m_out.at[pl.ds(p * GROUP, GROUP)], my_in.at[p], my_send.at[d], my_recv.at[d], along_y(p))
+
+    def mz_copy(d):
+        p = lax.rem(z + d, GROUP)
+        return remote(mz_out.at[p], mz_in.at[z], mz_send.at[d], mz_recv.at[d], along_z(p))
+
+    def mz_landed(d):
+        p = lax.rem(z + GROUP - d, GROUP)
+        return remote(mz_out.at[p], mz_in.at[p], mz_send.at[d], mz_recv.at[d], along_z(p))
+
+    others = range(1, GROUP)
+    for d in others:
+        az_copy(d).start()
     for n in range(CHUNKS // 2, CHUNKS):
         load(n).wait()
         lax.fori_loop(n * per_chunk, (n + 1) * per_chunk, contract, 0)
-    each(lambda d: a_landed(d).wait_recv())
-    each(lambda d: m_copy(d).start())
-    each(lambda d: a_copy(d).wait_send())
-    m_in[me] = m_out[me]
-
-    eliminate(a_ref, cols_ref, w_ref, lhs_ref, rhs_ref)
-
-    each(lambda d: m_landed(d).wait_recv())
-    total = jnp.sum(m_in[...], axis=0)
+    for d in others:
+        az_landed(d).wait_recv()
+    for d in others:
+        ay_copy(d).start()
+    for d in others:
+        my_copy(d).start()
+    my_in[column] = m_out[pl.ds(column * GROUP, GROUP)]
+    for d in others:
+        ay_landed(d).wait_recv()
+    for d in others:
+        az_copy(d).wait_send()
+        ay_copy(d).wait_send()
+
+    blocks = RANK // BLOCK
+    eliminate(0, blocks // 2, a_ref, cols_ref, w_ref, lhs_ref, rhs_ref)
+    for d in others:
+        my_landed(d).wait_recv()
+    mz_out[...] = jnp.sum(my_in[...], axis=0)
+    for d in others:
+        mz_copy(d).start()
+    mz_in[z] = mz_out[z]
+    eliminate(blocks // 2, blocks, a_ref, cols_ref, w_ref, lhs_ref, rhs_ref)
+    for d in others:
+        mz_landed(d).wait_recv()
+    total = jnp.sum(mz_in[...], axis=0)
     left, right = total[:4], total[4:]
     for h in range(2):
         part = jnp.dot(left, a_ref[h, pl.ds(0, LANES), :], precision=lax.Precision.HIGHEST,
@@ -265,7 +312,8 @@
         c_copy(d).wait_send()
         gb_copy(d).wait_send()
         gc_copy(d).wait_send()
-    each(lambda d: m_copy(d).wait_send())
+        my_copy(d).wait_send()
+        mz_copy(d).wait_send()
 
 
 def body(tensor, factor_b, factor_c):
@@ -276,8 +324,8 @@
         out_shape=jax.ShapeDtypeStruct((4, RANK), f32),
         in_specs=[
             pl.BlockSpec(memory_space=pl.ANY),
-            pl.BlockSpec(memory_space=pltpu.VMEM),
-            pl.BlockSpec(memory_space=pltpu.VMEM),
+            pl.BlockSpec(memory_space=pl.ANY),
+            pl.BlockSpec(memory_space=pl.ANY),
         ],
         out_specs=pl.BlockSpec(memory_space=pltpu.VMEM),
         scratch_shapes=[
@@ -292,18 +340,20 @@
             vmem((GROUP, SUB, LANES), f32),
             vmem((2, RANK, LANES), f32),
             vmem((PLANE, SUB, LANES), f32),
-            vmem((PLANE, SUB, LANES), f32),
+            vmem((GROUP, GROUP, SUB, LANES), f32),
+            vmem((GROUP, SUB, LANES), f32),
+            vmem((GROUP, SUB, LANES), f32),
             vmem((BLOCK, BLOCK, LANES), f32),
             vmem((2, BLOCK, LANES), f32),
             vmem((6 * BLOCK, RANK), bf16),
             vmem((6 * BLOCK, RANK), bf16),
+            dma((2,)),
             dma((CHUNKS,)),
-            *[dma((GROUP,)) for _ in range(8)],
-            *[dma((PLANE,)) for _ in range(4)],
+            *[dma((GROUP,)) for _ in range(16)],
         ],
         compiler_params=pltpu.CompilerParams(collective_id=0, has_side_effects=True),
         name="factor_update",
-    )(tensor, factor_b, factor_c)
+    )(tensor, factor_b.T, factor_c.T)
 
 
 def solution(mesh):

time: 54.8 us -> 48.2 us (0.88)
  Pallas kernels: 50.4 us -> 46.8 us
  local copies, waits for them, and re-layouts: 4.07 us -> 1.28 us
    pallas_call x1, Pallas kernels: 50.4 us -> 46.8 us  [body(): pl.pallas_call(kernel, out_shape=jax.ShapeDtypeStruct((4, RANK), f32), in...]
    unnamed x3 -> x1, local copies, waits for them, and re-layouts: 4.07 us -> 1.28 us
where the time goes in v2:
time: 48.2 us; the launch traced here: 48.1 us
  Pallas kernels  46.8 us (97%)
  local copies, waits for them, and re-layouts  1.28 us (3%)
    pallas_call x1, Pallas kernels, body(): pl.pallas_call(kernel, out_shape=jax.ShapeDtypeStruct((4, RANK), f32), in...  46.8 us
    unnamed x1, local copies, waits for them, and re-layouts  1.28 us

profile of v2, /device:TPU:1, one launch (start us, length us, event | category | flops | bytes accessed | tf_op | source)
XLA Modules:
  0.0 48.1 jit_solution(682123652072566252)
XLA Ops:
  0.0 46.8 %factor_update.1 = f32[4,256]{1,0:T(4,128)} custom-call(bf16[256,128,128]{2,1,0:T(8,128)(2,1)} %t_hbm.1, bf16[32,128]{1,0:T(8,128)(2,1)} %bitcast.2, bf16[32,128]{1,0:T(8,128)(2,1)} %bitcast.3), custom_call_target="tpu_custom_call" | custom-call | tf_op jit(solution)/shard_map/factor_update/pallas_call | solution.py:322
  46.8 1.3 %copy.5 = f32[4,256]{1,0:T(4,128)} copy(f32[4,256]{1,0:T(4,128)} %factor_update.1) | data formatting | bytes 8192

commit v3 on v2

--- a/solution.py
+++ b/solution.py
@@ -12,7 +12,8 @@
 RANK = 256
 LANES = 128
 SUB = 8
-BLOCK = 16
+PIV = 8
+HALF = LANES // PIV
 ROWS = 256
 DEPTH = 128
 STEP = 8
@@ -27,61 +28,91 @@
     return a, b, c
 
 
-def eliminate(first, last, a_ref, cols_ref, w_ref, lhs_ref, rhs_ref):
-    lane8 = lax.broadcasted_iota(jnp.int32, (SUB, LANES), 1)
+def lane(x, idx):
+    return jnp.take_along_axis(x, jnp.broadcast_to(idx, x.shape), axis=1)
+
+def start_sweep(a_ref, next_ref, w_ref, lhs_ref, rhs_ref):
+    lhs_ref[...] = jnp.zeros_like(lhs_ref)
+    rhs_ref[...] = jnp.zeros_like(rhs_ref)
+    for h in range(2):
+        next_ref[h] = a_ref[h, pl.ds(0, PIV), :]
+        w_ref[h] = a_ref[h, pl.ds(0, PIV), :]
+
+
+def trail(t, a_ref, w_ref, lhs_ref, rhs_ref):
     lane_n = lax.broadcasted_iota(jnp.int32, (RANK, LANES), 1)
+    change = jnp.dot(lhs_ref[...], rhs_ref[...], preferred_element_type=jnp.float32)
+    rows = pl.ds(pl.multiple_of(jnp.maximum(t, 0) * PIV, PIV), PIV)
+    for h in range(2):
+        lo = t * PIV - h * LANES
+        inside = (lane_n >= lo) & (lane_n < lo + PIV)
+        a_ref[h] = jnp.where(inside, 0.0, a_ref[h]) - change[:, h * LANES : (h + 1) * LANES]
+    for h in range(2):
+        a_ref[h, rows, :] = w_ref[h]
+
+
+def sweep(first, last, a_ref, next_ref, w_ref, lhs_ref, rhs_ref):
+    lane8 = lax.broadcasted_iota(jnp.int32, (PIV, LANES), 1)
+    row8 = lax.broadcasted_iota(jnp.int32, (PIV, LANES), 0)
+
+    def within(t, h):
+        lo = t * PIV - h * LANES
+        return (lane8 >= lo) & (lane8 < lo + PIV)
+
+    def spread(x, k):
+        return jnp.broadcast_to(x[k : k + 1], (PIV, LANES))
+
+    def less(rows, t, factors, w):
+        out = []
+        for h in range(2):
+            terms = [factors[k] * spread(w[h], k) for k in range(PIV)]
+            while len(terms) > 1:
+                terms = [p + q for p, q in zip(terms[::2], terms[1::2])]
+            out.append(jnp.where(within(t, h), 0.0, rows[h]) - terms[0])
+        return out
 
     def step(t, carry):
-        half = t // SUB
-        off = lax.rem(t, SUB) * BLOCK
-        rows = pl.ds(pl.multiple_of(t * BLOCK, BLOCK), BLOCK)
-        d = a_ref[half, rows, :]
-        d = pltpu.roll(d, lax.rem(LANES - off, LANES), 1)
-        for j in range(BLOCK):
-            cols_ref[j] = jnp.broadcast_to(d[:, j : j + 1], (BLOCK, LANES))
-        s, low, inv, y = {}, {}, [], []
-        for j in range(BLOCK):
-            for i in range(j, BLOCK):
-                s[i, j] = cols_ref[j, pl.ds(i, SUB, stride=0), :]
-        for i in range(BLOCK):
-            eye = jnp.where(lane8 == off + i, -1.0, 0.0)
-            row = []
+        half, off = t // HALF, lax.rem(t, HALF) * PIV
+        here = [next_ref[0], next_ref[1]]
+        d = jnp.where(half == 0, here[0], here[1])
+        s = [lane(d, off + j) for j in range(PIV)]
+        before = t - 1
+        ahead = pl.ds(pl.multiple_of(lax.rem(t + 1, RANK // PIV) * PIV, PIV), PIV)
+        base = [a_ref[h, ahead, :] for h in range(2)]
+        old = jnp.where(before < HALF, base[0], base[1])
+        old_off = lax.rem(before + HALF, HALF) * PIV
+        factors = [jnp.where(t > 0, lane(old, old_off + k), 0.0) for k in range(PIV)]
+        base = less(base, before, factors, [w_ref[0], w_ref[1]])
+        c = jnp.where(half == 0, base[0], base[1])
+        factors = [lane(c, off + k) for k in range(PIV)]
+        trail(before, a_ref, w_ref, lhs_ref, rhs_ref)
+        for h in range(2):
+            r1, r2, r3 = split3(here[h])
+            lhs_ref[h * LANES : (h + 1) * LANES, :] = jnp.concatenate([r1, r1, r2, r2, r1, r3], axis=0).T
+        y = []
+        for h in range(2):
+            eye = jnp.where(lane8 == t * PIV - h * LANES + row8, -1.0, 0.0)
+            y.append(jnp.where(within(t, h), eye, here[h]))
+        scale = None
+        for k in range(PIV):
+            inv = pltpu.reciprocal(spread(s[k], k))
+            scale = inv if k == 0 else jnp.where(row8 == k, inv, scale)
+            away = jnp.where(row8 == k, 0.0, s[k])
+            m = away * inv
+            for j in range(k + 1, PIV):
+                if j == k + 1:
+                    s[j] = s[j] - (away * spread(s[j], k)) * inv
+                else:
+                    s[j] = s[j] - m * spread(s[j], k)
             for h in range(2):
-                inside = (lane8 >= off) & (lane8 < off + BLOCK) & (half == h)
-                row.append(jnp.where(inside, eye, a_ref[h, pl.ds(t * BLOCK + i, SUB, stride=0), :]))
-            y.append(row)
-        for k in range(BLOCK):
-            inv.append(pltpu.reciprocal(s[k, k]))
-            for j in range(k + 1, BLOCK):
-                low[j, k] = s[j, k] * inv[k]
-            for j in range(k + 1, BLOCK):
-                for i in range(j, BLOCK):
-                    s[i, j] = s[i, j] - low[i, k] * s[j, k]
-                for h in range(2):
-                    y[j][h] = y[j][h] - low[j, k] * y[k][h]
-        for k in range(BLOCK):
-            for h in range(2):
-                y[k][h] = y[k][h] * inv[k]
-        for k in range(BLOCK - 1, -1, -1):
-            for h in range(2):
-                w_ref[h, k : k + 1, :] = y[k][h][0:1]
-            for j in range(k):
-                for h in range(2):
-                    y[j][h] = y[j][h] - low[k, j] * y[k][h]
+                y[h] = y[h] - m * spread(y[h], k)
+        w = [y[h] * scale for h in range(2)]
+        after = less(base, t, factors, w)
         for h in range(2):
-            lanes = pl.ds(h * LANES, LANES)
-            r1, r2, r3 = split3(a_ref[h, rows, :])
-            lhs_ref[:, lanes] = jnp.concatenate([r1, r1, r2, r2, r1, r3], axis=0)
-            w1, w2, w3 = split3(w_ref[h])
-            rhs_ref[:, lanes] = jnp.concatenate([w1, w2, w1, w2, w3, w1], axis=0)
-        change = lax.dot_general(
-            lhs_ref[...], rhs_ref[...], (((0,), (0,)), ((), ())), preferred_element_type=jnp.float32
-        )
-        for h in range(2):
-            inside = (lane_n >= off) & (lane_n < off + BLOCK) & (half == h)
-            a_ref[h] = jnp.where(inside, 0.0, a_ref[h]) - change[:, h * LANES : (h + 1) * LANES]
-        for h in range(2):
-            a_ref[h, rows, :] = w_ref[h]
+            next_ref[h] = after[h]
+            w_ref[h] = w[h]
+            w1, w2, w3 = split3(w[h])
+            rhs_ref[:, h * LANES : (h + 1) * LANES] = jnp.concatenate([w1, w2, w1, w2, w3, w1], axis=0)
         return carry
 
     lax.fori_loop(first, last, step, 0)
@@ -90,7 +121,7 @@
 def kernel(
     t_hbm, fb_hbm, fc_hbm, out_ref,
     t_buf, b_buf, c_buf, b_wide, c_wide, gb, gc, gb_in, gc_in, a_ref, m_out, my_in, mz_out, mz_in,
-    cols_ref, w_ref, lhs_ref, rhs_ref,
+    next_ref, w_ref, lhs_ref, rhs_ref,
     f_sem, t_sem, b_send, b_recv, c_send, c_recv, gb_send, gb_recv, gc_send, gc_recv,
     az_send, az_recv, ay_send, ay_recv, my_send, my_recv, mz_send, mz_recv,
 ):
@@ -209,11 +240,14 @@
         m_out[tile_of(j, k + 1)] = jnp.concatenate([left[4:], right[4:]], axis=0)
         return carry
 
-    steps = ROWS // STEP
-    per_chunk = steps // CHUNKS
-    for n in range(CHUNKS // 2):
-        load(n).wait()
-        lax.fori_loop(n * per_chunk, (n + 1) * per_chunk, contract, 0)
+    per_chunk = ROWS // STEP // CHUNKS
+
+    def contract_chunks(first, last):
+        for n in range(first, last):
+            load(n).wait()
+        lax.fori_loop(first * per_chunk, last * per_chunk, contract, 0)
+
+    contract_chunks(0, 3)
 
     for d in range(1, GROUP):
         gb_landed(d).wait_recv()
@@ -271,13 +305,12 @@
     others = range(1, GROUP)
     for d in others:
         az_copy(d).start()
-    for n in range(CHUNKS // 2, CHUNKS):
-        load(n).wait()
-        lax.fori_loop(n * per_chunk, (n + 1) * per_chunk, contract, 0)
+    contract_chunks(3, 5)
     for d in others:
         az_landed(d).wait_recv()
     for d in others:
         ay_copy(d).start()
+    contract_chunks(5, CHUNKS)
     for d in others:
         my_copy(d).start()
     my_in[column] = m_out[pl.ds(column * GROUP, GROUP)]
@@ -287,15 +320,17 @@
         az_copy(d).wait_send()
         ay_copy(d).wait_send()
 
-    blocks = RANK // BLOCK
-    eliminate(0, blocks // 2, a_ref, cols_ref, w_ref, lhs_ref, rhs_ref)
+    blocks = RANK // PIV
+    start_sweep(a_ref, next_ref, w_ref, lhs_ref, rhs_ref)
+    sweep(0, blocks // 2, a_ref, next_ref, w_ref, lhs_ref, rhs_ref)
     for d in others:
         my_landed(d).wait_recv()
     mz_out[...] = jnp.sum(my_in[...], axis=0)
     for d in others:
         mz_copy(d).start()
     mz_in[z] = mz_out[z]
-    eliminate(blocks // 2, blocks, a_ref, cols_ref, w_ref, lhs_ref, rhs_ref)
+    sweep(blocks // 2, blocks, a_ref, next_ref, w_ref, lhs_ref, rhs_ref)
+    trail(blocks - 1, a_ref, w_ref, lhs_ref, rhs_ref)
     for d in others:
         mz_landed(d).wait_recv()
     total = jnp.sum(mz_in[...], axis=0)
@@ -343,10 +378,10 @@
             vmem((GROUP, GROUP, SUB, LANES), f32),
             vmem((GROUP, SUB, LANES), f32),
             vmem((GROUP, SUB, LANES), f32),
-            vmem((BLOCK, BLOCK, LANES), f32),
-            vmem((2, BLOCK, LANES), f32),
-            vmem((6 * BLOCK, RANK), bf16),
-            vmem((6 * BLOCK, RANK), bf16),
+            vmem((2, PIV, LANES), f32),
+            vmem((2, PIV, LANES), f32),
+            vmem((RANK, 6 * PIV), bf16),
+            vmem((6 * PIV, RANK), bf16),
             dma((2,)),
             dma((CHUNKS,)),
             *[dma((GROUP,)) for _ in range(16)],

time: 48.2 us -> 42.2 us (0.88)
  Pallas kernels: 46.8 us -> 40.8 us
    pallas_call x1, Pallas kernels: 46.8 us -> 40.8 us  [body(): pl.pallas_call(kernel, out_shape=jax.ShapeDtypeStruct((4, RANK), f32), in...]
where the time goes in v3:
time: 42.2 us; the launch traced here: 42.1 us
  Pallas kernels  40.8 us (97%)
  local copies, waits for them, and re-layouts  1.28 us (3%)
    pallas_call x1, Pallas kernels, body(): pl.pallas_call(kernel, out_shape=jax.ShapeDtypeStruct((4, RANK), f32), in...  40.8 us
    unnamed x1, local copies, waits for them, and re-layouts  1.28 us

profile of v3, /device:TPU:1, one launch (start us, length us, event | category | flops | bytes accessed | tf_op | source)
XLA Modules:
  0.0 42.1 jit_solution(14720034514117345175)
XLA Ops:
  0.0 40.8 %factor_update.1 = f32[4,256]{1,0:T(4,128)} custom-call(bf16[256,128,128]{2,1,0:T(8,128)(2,1)} %t_hbm.1, bf16[32,128]{1,0:T(8,128)(2,1)} %bitcast.2, bf16[32,128]{1,0:T(8,128)(2,1)} %bitcast.3), custom_call_target="tpu_custom_call" | custom-call | tf_op jit(solution)/shard_map/factor_update/pallas_call | solution.py:357
  40.8 1.3 %copy.5 = f32[4,256]{1,0:T(4,128)} copy(f32[4,256]{1,0:T(4,128)} %factor_update.1) | data formatting | bytes 8192

commit v4 on v3

--- a/solution.py
+++ b/solution.py
@@ -12,7 +12,7 @@
 RANK = 256
 LANES = 128
 SUB = 8
-PIV = 8
+PIV = 16
 HALF = LANES // PIV
 ROWS = 256
 DEPTH = 128
@@ -31,6 +31,7 @@
 def lane(x, idx):
     return jnp.take_along_axis(x, jnp.broadcast_to(idx, x.shape), axis=1)
 
+
 def start_sweep(a_ref, next_ref, w_ref, lhs_ref, rhs_ref):
     lhs_ref[...] = jnp.zeros_like(lhs_ref)
     rhs_ref[...] = jnp.zeros_like(rhs_ref)
@@ -52,66 +53,68 @@
 
 
 def sweep(first, last, a_ref, next_ref, w_ref, lhs_ref, rhs_ref):
-    lane8 = lax.broadcasted_iota(jnp.int32, (PIV, LANES), 1)
-    row8 = lax.broadcasted_iota(jnp.int32, (PIV, LANES), 0)
-
-    def within(t, h):
-        lo = t * PIV - h * LANES
-        return (lane8 >= lo) & (lane8 < lo + PIV)
+    lane8 = lax.broadcasted_iota(jnp.int32, (SUB, LANES), 1)
+    row8 = lax.broadcasted_iota(jnp.int32, (SUB, LANES), 0)
+    lane16 = lax.broadcasted_iota(jnp.int32, (PIV, LANES), 1)
+    groups = range(PIV // SUB)
 
     def spread(x, k):
-        return jnp.broadcast_to(x[k : k + 1], (PIV, LANES))
-
-    def less(rows, t, factors, w):
-        out = []
-        for h in range(2):
-            terms = [factors[k] * spread(w[h], k) for k in range(PIV)]
-            while len(terms) > 1:
-                terms = [p + q for p, q in zip(terms[::2], terms[1::2])]
-            out.append(jnp.where(within(t, h), 0.0, rows[h]) - terms[0])
-        return out
+        return jnp.broadcast_to(x[k // SUB][k % SUB : k % SUB + 1], (SUB, LANES))
 
     def step(t, carry):
         half, off = t // HALF, lax.rem(t, HALF) * PIV
-        here = [next_ref[0], next_ref[1]]
-        d = jnp.where(half == 0, here[0], here[1])
-        s = [lane(d, off + j) for j in range(PIV)]
-        before = t - 1
+        here = [[next_ref[h, g * SUB : (g + 1) * SUB, :] for g in groups] for h in range(2)]
+        d = [jnp.where(half == 0, here[0][g], here[1][g]) for g in groups]
+        s = [[lane(d[g], off + j) for g in groups] for j in range(PIV)]
         ahead = pl.ds(pl.multiple_of(lax.rem(t + 1, RANK // PIV) * PIV, PIV), PIV)
-        base = [a_ref[h, ahead, :] for h in range(2)]
-        old = jnp.where(before < HALF, base[0], base[1])
-        old_off = lax.rem(before + HALF, HALF) * PIV
-        factors = [jnp.where(t > 0, lane(old, old_off + k), 0.0) for k in range(PIV)]
-        base = less(base, before, factors, [w_ref[0], w_ref[1]])
+        change = jnp.dot(lhs_ref[ahead, :], rhs_ref[...], preferred_element_type=jnp.float32)
+        base = []
+        for h in range(2):
+            lo = (t - 1) * PIV - h * LANES
+            inside = (lane16 >= lo) & (lane16 < lo + PIV)
+            base.append(jnp.where(inside, 0.0, a_ref[h, ahead, :]) - change[:, h * LANES : (h + 1) * LANES])
         c = jnp.where(half == 0, base[0], base[1])
-        factors = [lane(c, off + k) for k in range(PIV)]
-        trail(before, a_ref, w_ref, lhs_ref, rhs_ref)
+        factors = [[lane(c[g * SUB : (g + 1) * SUB], off + k) for k in range(PIV)] for g in groups]
+        trail(t - 1, a_ref, w_ref, lhs_ref, rhs_ref)
         for h in range(2):
-            r1, r2, r3 = split3(here[h])
+            r1, r2, r3 = split3(next_ref[h])
             lhs_ref[h * LANES : (h + 1) * LANES, :] = jnp.concatenate([r1, r1, r2, r2, r1, r3], axis=0).T
         y = []
         for h in range(2):
-            eye = jnp.where(lane8 == t * PIV - h * LANES + row8, -1.0, 0.0)
-            y.append(jnp.where(within(t, h), eye, here[h]))
-        scale = None
+            lo = t * PIV - h * LANES
+            inside = (lane8 >= lo) & (lane8 < lo + PIV)
+            y.append([
+                jnp.where(inside, jnp.where(lane8 == lo + g * SUB + row8, -1.0, 0.0), here[h][g]) for g in groups
+            ])
+        scale = [None for _ in groups]
         for k in range(PIV):
             inv = pltpu.reciprocal(spread(s[k], k))
-            scale = inv if k == 0 else jnp.where(row8 == k, inv, scale)
-            away = jnp.where(row8 == k, 0.0, s[k])
-            m = away * inv
+            g0, r0 = k // SUB, k % SUB
+            scale[g0] = inv if r0 == 0 else jnp.where(row8 == r0, inv, scale[g0])
+            away = [jnp.where(row8 == r0, 0.0, s[k][g]) if g == g0 else s[k][g] for g in groups]
+            m = [away[g] * inv for g in groups]
             for j in range(k + 1, PIV):
+                sj = spread(s[j], k)
                 if j == k + 1:
-                    s[j] = s[j] - (away * spread(s[j], k)) * inv
+                    s[j] = [s[j][g] - (away[g] * sj) * inv for g in groups]
                 else:
-                    s[j] = s[j] - m * spread(s[j], k)
+                    s[j] = [s[j][g] - m[g] * sj for g in groups]
             for h in range(2):
-                y[h] = y[h] - m * spread(y[h], k)
-        w = [y[h] * scale for h in range(2)]
-        after = less(base, t, factors, w)
+                yk = spread(y[h], k)
+                y[h] = [y[h][g] - m[g] * yk for g in groups]
+        w = [[y[h][g] * scale[g] for g in groups] for h in range(2)]
+        for g in groups:
+            for h in range(2):
+                terms = [factors[g][k] * spread(w[h], k) for k in range(PIV)]
+                while len(terms) > 1:
+                    terms = [p + q for p, q in zip(terms[::2], terms[1::2])]
+                lo = t * PIV - h * LANES
+                inside = (lane8 >= lo) & (lane8 < lo + PIV)
+                next_ref[h, g * SUB : (g + 1) * SUB, :] = jnp.where(inside, 0.0, base[h][g * SUB : (g + 1) * SUB]) - terms[0]
         for h in range(2):
-            next_ref[h] = after[h]
-            w_ref[h] = w[h]
-            w1, w2, w3 = split3(w[h])
+            full = jnp.concatenate(w[h], axis=0)
+            w_ref[h] = full
+            w1, w2, w3 = split3(full)
             rhs_ref[:, h * LANES : (h + 1) * LANES] = jnp.concatenate([w1, w2, w1, w2, w3, w1], axis=0)
         return carry
 
@@ -149,7 +152,8 @@
     load_c = pltpu.make_async_copy(fc_hbm, c_buf.at[ja], f_sem.at[1])
     load_b.start()
     load_c.start()
-    for n in range(CHUNKS):
+    order = [lax.rem(y + d, 4) + 4 * e for d in (2, 1, 3, 0) for e in range(2)]
+    for n in order:
         load(n).start()
 
     barrier = pltpu.get_barrier_semaphore()
@@ -242,12 +246,30 @@
 
     per_chunk = ROWS // STEP // CHUNKS
 
-    def contract_chunks(first, last):
-        for n in range(first, last):
-            load(n).wait()
-        lax.fori_loop(first * per_chunk, last * per_chunk, contract, 0)
-
-    contract_chunks(0, 3)
+    def contract_chunk(n):
+        load(n).wait()
+        lax.fori_loop(0, per_chunk, lambda i, carry: contract(n * per_chunk + i, carry), 0)
+
+    def my_column(dy, e):
+        return lax.rem(y + dy, 4) * 2 + (core if e == 0 else 1 - core)
+
+    def my_copy(dy, e):
+        p, k = my_column(dy, e), dy * 2 + e
+        return remote(
+            m_out.at[pl.ds(p * GROUP, GROUP)], my_in.at[column], my_send.at[k], my_recv.at[k], along_y(p)
+        )
+
+    def my_landed(dy, e):
+        p, k = my_column(4 - dy, e), dy * 2 + e
+        return remote(m_out.at[pl.ds(p * GROUP, GROUP)], my_in.at[p], my_send.at[k], my_recv.at[k], along_y(p))
+
+    my_all = [(dy, e) for dy in range(4) for e in range(2) if dy + e > 0]
+
+    contract_chunk(order[0])
+    contract_chunk(order[1])
+    my_copy(2, 0).start()
+    my_copy(2, 1).start()
+    contract_chunk(order[2])
 
     for d in range(1, GROUP):
         gb_landed(d).wait_recv()
@@ -284,16 +306,6 @@
         p = lax.rem(column + GROUP - d, GROUP)
         return remote(part(a_ref, p), part(a_ref, p), ay_send.at[d], ay_recv.at[d], along_y(p))
 
-    def my_copy(d):
-        p = lax.rem(column + d, GROUP)
-        return remote(
-            m_out.at[pl.ds(p * GROUP, GROUP)], my_in.at[column], my_send.at[d], my_recv.at[d], along_y(p)
-        )
-
-    def my_landed(d):
-        p = lax.rem(column + GROUP - d, GROUP)
-        return remote(m_out.at[pl.ds(p * GROUP, GROUP)], my_in.at[p], my_send.at[d], my_recv.at[d], along_y(p))
-
     def mz_copy(d):
         p = lax.rem(z + d, GROUP)
         return remote(mz_out.at[p], mz_in.at[z], mz_send.at[d], mz_recv.at[d], along_z(p))
@@ -305,14 +317,20 @@
     others = range(1, GROUP)
     for d in others:
         az_copy(d).start()
-    contract_chunks(3, 5)
+    contract_chunk(order[3])
+    my_copy(1, 0).start()
+    my_copy(1, 1).start()
+    contract_chunk(order[4])
+    contract_chunk(order[5])
+    my_copy(3, 0).start()
+    my_copy(3, 1).start()
     for d in others:
         az_landed(d).wait_recv()
     for d in others:
         ay_copy(d).start()
-    contract_chunks(5, CHUNKS)
-    for d in others:
-        my_copy(d).start()
+    contract_chunk(order[6])
+    contract_chunk(order[7])
+    my_copy(0, 1).start()
     my_in[column] = m_out[pl.ds(column * GROUP, GROUP)]
     for d in others:
         ay_landed(d).wait_recv()
@@ -322,14 +340,14 @@
 
     blocks = RANK // PIV
     start_sweep(a_ref, next_ref, w_ref, lhs_ref, rhs_ref)
-    sweep(0, blocks // 2, a_ref, next_ref, w_ref, lhs_ref, rhs_ref)
-    for d in others:
-        my_landed(d).wait_recv()
+    sweep(0, 4, a_ref, next_ref, w_ref, lhs_ref, rhs_ref)
+    for dy, e in my_all:
+        my_landed(dy, e).wait_recv()
     mz_out[...] = jnp.sum(my_in[...], axis=0)
     for d in others:
         mz_copy(d).start()
     mz_in[z] = mz_out[z]
-    sweep(blocks // 2, blocks, a_ref, next_ref, w_ref, lhs_ref, rhs_ref)
+    sweep(4, blocks, a_ref, next_ref, w_ref, lhs_ref, rhs_ref)
     trail(blocks - 1, a_ref, w_ref, lhs_ref, rhs_ref)
     for d in others:
         mz_landed(d).wait_recv()
@@ -347,8 +365,9 @@
         c_copy(d).wait_send()
         gb_copy(d).wait_send()
         gc_copy(d).wait_send()
-        my_copy(d).wait_send()
         mz_copy(d).wait_send()
+    for dy, e in my_all:
+        my_copy(dy, e).wait_send()
 
 
 def body(tensor, factor_b, factor_c):

time: 42.2 us -> 39.7 us (0.941)
  Pallas kernels: 40.8 us -> 38.3 us
    pallas_call x1, Pallas kernels: 40.8 us -> 38.3 us  [body(): pl.pallas_call(kernel, out_shape=jax.ShapeDtypeStruct((4, RANK), f32), in...]
where the time goes in v4:
time: 39.7 us; the launch traced here: 39.6 us
  Pallas kernels  38.3 us (96%)
  local copies, waits for them, and re-layouts  1.28 us (3%)
    pallas_call x1, Pallas kernels, body(): pl.pallas_call(kernel, out_shape=jax.ShapeDtypeStruct((4, RANK), f32), in...  38.3 us
    unnamed x1, local copies, waits for them, and re-layouts  1.28 us

profile of v4, /device:TPU:1, one launch (start us, length us, event | category | flops | bytes accessed | tf_op | source)
XLA Modules:
  0.0 39.6 jit_solution(17386059468685186918)
XLA Ops:
  0.0 38.3 %factor_update.1 = f32[4,256]{1,0:T(4,128)} custom-call(bf16[256,128,128]{2,1,0:T(8,128)(2,1)} %t_hbm.1, bf16[32,128]{1,0:T(8,128)(2,1)} %bitcast.2, bf16[32,128]{1,0:T(8,128)(2,1)} %bitcast.3), custom_call_target="tpu_custom_call" | custom-call | tf_op jit(solution)/shard_map/factor_update/pallas_call | solution.py:376
  38.3 1.3 %copy.5 = f32[4,256]{1,0:T(4,128)} copy(f32[4,256]{1,0:T(4,128)} %factor_update.1) | data formatting | bytes 8192

commit v5 on v4

--- a/solution.py
+++ b/solution.py
@@ -215,21 +215,23 @@
     for d in range(1, GROUP):
         c_landed(d).wait_recv()
     ct = c_buf[...].reshape(RANK, DEPTH)
-    gram = lax.dot_general(ct, ct, nt, preferred_element_type=jnp.float32)
-    for h in range(2):
-        gc[pl.ds(h * 32, 32)] = gram[:, h * LANES : (h + 1) * LANES].reshape(32, SUB, LANES)
+    first = lax.rem(y, 2) * 4 + ja // 4
+    run = jnp.concatenate([c_buf[first], c_buf[first + 2]], axis=0)
+    side = c_buf[pl.ds((y // 2) * 4, 4)].reshape(LANES, DEPTH)
+    gram = lax.dot_general(run, side, nt, preferred_element_type=jnp.float32)
+    gc[...] = gram.reshape(GROUP, SUB, LANES)
 
     def gc_copy(d):
         q = lax.rem(ka + d, GROUP)
-        return remote(gc.at[tile_of(ja, q)], gc_in.at[ka], gc_send.at[d], gc_recv.at[d], {"ka": q})
+        return remote(gc.at[lax.rem(q, 2) * 4 + q // 2], gc_in.at[ka], gc_send.at[d], gc_recv.at[d], {"ka": q})
 
     def gc_landed(d):
         q = lax.rem(ka + GROUP - d, GROUP)
-        return remote(gc.at[tile_of(ja, q)], gc_in.at[q], gc_send.at[d], gc_recv.at[d], {"ka": q})
+        return remote(gc.at[lax.rem(q, 2) * 4 + q // 2], gc_in.at[q], gc_send.at[d], gc_recv.at[d], {"ka": q})
 
     for d in range(1, GROUP):
         gc_copy(d).start()
-    gc_in[ka] = gc[me]
+    gc_in[ka] = gc[core * 4 + ka // 2]
 
     b_wide[...] = bt.astype(jnp.float32).T
     c_wide[...] = ct.astype(jnp.float32).T.astype(jnp.bfloat16)
@@ -283,28 +285,30 @@
     mine = pl.ds(pl.multiple_of(my_row, SUB), SUB)
     a_ref[my_half, mine, :] = sum_b * sum_c + jnp.where(row == col, RIDGE, 0.0)
 
-    def part(ref, p):
-        return ref.at[p // 4, pl.ds(pl.multiple_of(lax.rem(p, 4) * 64, 64), 64), :]
-
-    def az_tile(p):
-        start = lax.rem(column, 4) * 64 + p * SUB
-        return a_ref.at[column // 4, pl.ds(pl.multiple_of(start, SUB), SUB), :]
-
-    def az_copy(d):
-        return remote(az_tile(z), az_tile(z), az_send.at[d], az_recv.at[d], along_z(lax.rem(z + d, GROUP)))
-
-    def az_landed(d):
-        p = lax.rem(z + GROUP - d, GROUP)
-        return remote(az_tile(p), az_tile(p), az_send.at[d], az_recv.at[d], along_z(p))
-
-    def ay_copy(d):
-        return remote(
-            part(a_ref, column), part(a_ref, column), ay_send.at[d], ay_recv.at[d], along_y(lax.rem(column + d, GROUP))
-        )
-
-    def ay_landed(d):
+    def rows_of(p, q, count):
+        start = lax.rem(p, 4) * 64 + q * SUB
+        return a_ref.at[p // 4, pl.ds(pl.multiple_of(start, SUB), count * SUB), :]
+
+    def z_at(e, d):
+        return lax.rem(z // 4 + e, 2) * 4 + lax.rem(z + d, 4)
+
+    def az_copy(e, d):
+        tile, k = rows_of(column, z, 1), e * 4 + d
+        return remote(tile, tile, az_send.at[k], az_recv.at[k], along_z(z_at(e, d)))
+
+    def az_landed(e, d):
+        q, k = z_at(e, 4 - d), e * 4 + d
+        tile = rows_of(column, q, 1)
+        return remote(tile, tile, az_send.at[k], az_recv.at[k], along_z(q))
+
+    def ay_copy(e, d):
+        tiles = rows_of(column, lax.rem(z // 4 + e, 2) * 4, 4)
+        return remote(tiles, tiles, ay_send.at[e, d], ay_recv.at[e, d], along_y(lax.rem(column + d, GROUP)))
+
+    def ay_landed(e, d):
         p = lax.rem(column + GROUP - d, GROUP)
-        return remote(part(a_ref, p), part(a_ref, p), ay_send.at[d], ay_recv.at[d], along_y(p))
+        tiles = rows_of(p, lax.rem(z // 4 + e, 2) * 4, 4)
+        return remote(tiles, tiles, ay_send.at[e, d], ay_recv.at[e, d], along_y(p))
 
     def mz_copy(d):
         p = lax.rem(z + d, GROUP)
@@ -315,28 +319,38 @@
         return remote(mz_out.at[p], mz_in.at[p], mz_send.at[d], mz_recv.at[d], along_z(p))
 
     others = range(1, GROUP)
-    for d in others:
-        az_copy(d).start()
+    az_all = [(e, d) for e in (1, 0) for d in range(4) if e + d > 0]
+
+    def pass_on(e):
+        for d in range(4):
+            if e + d > 0:
+                az_landed(e, d).wait_recv()
+        for d in others:
+            ay_copy(e, d).start()
+
+    for e, d in az_all:
+        az_copy(e, d).start()
     contract_chunk(order[3])
     my_copy(1, 0).start()
     my_copy(1, 1).start()
     contract_chunk(order[4])
+    pass_on(0)
     contract_chunk(order[5])
+    pass_on(1)
     my_copy(3, 0).start()
     my_copy(3, 1).start()
-    for d in others:
-        az_landed(d).wait_recv()
-    for d in others:
-        ay_copy(d).start()
     contract_chunk(order[6])
     contract_chunk(order[7])
     my_copy(0, 1).start()
     my_in[column] = m_out[pl.ds(column * GROUP, GROUP)]
     for d in others:
-        ay_landed(d).wait_recv()
+        for e in range(2):
+            ay_landed(e, d).wait_recv()
     for d in others:
-        az_copy(d).wait_send()
-        ay_copy(d).wait_send()
+        for e in range(2):
+            ay_copy(e, d).wait_send()
+    for e, d in az_all:
+        az_copy(e, d).wait_send()
 
     blocks = RANK // PIV
     start_sweep(a_ref, next_ref, w_ref, lhs_ref, rhs_ref)
@@ -389,7 +403,7 @@
             vmem((DEPTH, RANK), f32),
             vmem((DEPTH, RANK), bf16),
             vmem((PLANE, SUB, LANES), f32),
-            vmem((PLANE, SUB, LANES), f32),
+            vmem((GROUP, SUB, LANES), f32),
             vmem((GROUP, SUB, LANES), f32),
             vmem((GROUP, SUB, LANES), f32),
             vmem((2, RANK, LANES), f32),
@@ -403,7 +417,9 @@
             vmem((6 * PIV, RANK), bf16),
             dma((2,)),
             dma((CHUNKS,)),
-            *[dma((GROUP,)) for _ in range(16)],
+            *[dma((GROUP,)) for _ in range(10)],
+            *[dma((2, GROUP)) for _ in range(2)],
+            *[dma((GROUP,)) for _ in range(4)],
         ],
         compiler_params=pltpu.CompilerParams(collective_id=0, has_side_effects=True),
         name="factor_update",

time: 39.7 us -> 39.4 us (level)
  no operation moved by 1% of the time
where the time goes in v5:
time: 39.4 us; the launch traced here: 39.3 us
  Pallas kernels  38 us (96%)
  local copies, waits for them, and re-layouts  1.28 us (3%)
    pallas_call x1, Pallas kernels, body(): pl.pallas_call(kernel, out_shape=jax.ShapeDtypeStruct((4, RANK), f32), in...  38 us
    unnamed x1, local copies, waits for them, and re-layouts  1.28 us

profile of v5, /device:TPU:1, one launch (start us, length us, event | category | flops | bytes accessed | tf_op | source)
XLA Modules:
  0.0 39.3 jit_solution(12799229771671313017)
XLA Ops:
  0.0 38.0 %factor_update.1 = f32[4,256]{1,0:T(4,128)} custom-call(bf16[256,128,128]{2,1,0:T(8,128)(2,1)} %t_hbm.1, bf16[32,128]{1,0:T(8,128)(2,1)} %bitcast.2, bf16[32,128]{1,0:T(8,128)(2,1)} %bitcast.3), custom_call_target="tpu_custom_call" | custom-call | tf_op jit(solution)/shard_map/factor_update/pallas_call | solution.py:390
  38.0 1.3 %copy.5 = f32[4,256]{1,0:T(4,128)} copy(f32[4,256]{1,0:T(4,128)} %factor_update.1) | data formatting | bytes 8192

commit v6 on v5

--- a/solution.py
+++ b/solution.py
@@ -190,6 +190,7 @@
 
     for d in range(1, GROUP):
         c_copy(d).start()
+    for d in range(1, GROUP):
         b_copy(d).start()
 
     for d in range(1, GROUP):
@@ -354,14 +355,14 @@
 
     blocks = RANK // PIV
     start_sweep(a_ref, next_ref, w_ref, lhs_ref, rhs_ref)
-    sweep(0, 4, a_ref, next_ref, w_ref, lhs_ref, rhs_ref)
+    sweep(0, 3, a_ref, next_ref, w_ref, lhs_ref, rhs_ref)
     for dy, e in my_all:
         my_landed(dy, e).wait_recv()
     mz_out[...] = jnp.sum(my_in[...], axis=0)
     for d in others:
         mz_copy(d).start()
     mz_in[z] = mz_out[z]
-    sweep(4, blocks, a_ref, next_ref, w_ref, lhs_ref, rhs_ref)
+    sweep(3, blocks, a_ref, next_ref, w_ref, lhs_ref, rhs_ref)
     trail(blocks - 1, a_ref, w_ref, lhs_ref, rhs_ref)
     for d in others:
         mz_landed(d).wait_recv()

time: 39.4 us -> 38.9 us (0.987)
  Pallas kernels: 38 us -> 37.5 us
    pallas_call x1, Pallas kernels: 38 us -> 37.5 us  [body(): pl.pallas_call(kernel, out_shape=jax.ShapeDtypeStruct((4, RANK), f32), in...]
where the time goes in v6:
time: 38.9 us; the launch traced here: 38.8 us
  Pallas kernels  37.5 us (96%)
  local copies, waits for them, and re-layouts  1.28 us (3%)
    pallas_call x1, Pallas kernels, body(): pl.pallas_call(kernel, out_shape=jax.ShapeDtypeStruct((4, RANK), f32), in...  37.5 us
    unnamed x1, local copies, waits for them, and re-layouts  1.28 us

profile of v6, /device:TPU:1, one launch (start us, length us, event | category | flops | bytes accessed | tf_op | source)
XLA Modules:
  0.0 38.8 jit_solution(2827027610641233034)
XLA Ops:
  0.0 37.5 %factor_update.1 = f32[4,256]{1,0:T(4,128)} custom-call(bf16[256,128,128]{2,1,0:T(8,128)(2,1)} %t_hbm.1, bf16[32,128]{1,0:T(8,128)(2,1)} %bitcast.2, bf16[32,128]{1,0:T(8,128)(2,1)} %bitcast.3), custom_call_target="tpu_custom_call" | custom-call | tf_op jit(solution)/shard_map/factor_update/pallas_call | solution.py:391
  37.5 1.3 %copy.5 = f32[4,256]{1,0:T(4,128)} copy(f32[4,256]{1,0:T(4,128)} %factor_update.1) | data formatting | bytes 8192
